TPU v7x, 32 devices: a whole 2x2x4 slice. The times are simulated.
32 devices in a mesh: cg: 8 (over z, x), vg: 4 (over y, core).
Axes of the slice: x: 2, y: 2, z: 4, core: 2. Of those that a mesh axis runs over, the one named last changes fastest.
Arguments:
- con_embed: float32 [32768, 128], P(('cg', 'vg')), may hold values from -6 to 6
- var_embed: float32 [32768, 128], P(('vg', 'cg')), may hold values from -6 to 6
- row_coef: float32 [32768], P(('cg', 'vg')), may hold values from 0.3 to 3
- col_coef: float32 [32768], P(('vg', 'cg')), may hold values from 0.3 to 3
- self_weight: float32 [128, 128], replicated, may hold values from -0.5 to 0.5
- msg_weight: float32 [128, 128], replicated, may hold values from -0.0234375 to 0.0234375
- timestep: int32 [1], replicated, may hold values from 0 to 999
- tile_rows: int32 [8, 4, 16], P('cg', 'vg'), may hold values from 0 to 7, as said below
- tile_cols: int32 [8, 4, 16], P('cg', 'vg'), may hold values from 0 to 15, as said below
- pattern: bfloat16 [8, 4, 16, 512, 512], P('cg', 'vg'), may hold values from -6 to 6
- cotangent: float32 [32768, 128], P(('cg', 'vg')), may hold values from -6 to 6
Outputs:
- con_update: float32 [32768, 128], P(('cg', 'vg'))
- grad_con: float32 [32768, 128], P(('cg', 'vg'))
- grad_var: float32 [32768, 128], P(('vg', 'cg'))
- grad_msg: float32 [128, 128], replicated
- grad_self: float32 [128, 128], replicated
Inputs may be any that keep to these rules, and one draw needn't show every extreme that they name: `tile_rows`: every device lists tile row 0 and tile row 7; a device lists distinct tiles unless 16 exceeds 8 * 16, and repeated tiles add. `tile_cols`: every device lists tile column 0 and tile column 15, together with the rows above: tiles (0, 0) and (7, 15) are on every list.
All inputs are finite; a program needn't handle non-finite values.
Results may differ from a plain program's by a relative error of at most 0.007.
Values may be sent and summed in bfloat16 or wider, within the bound.
A program may use at most 128 MiB of HBM per device.

v0:
```python
import math
import jax
import jax.numpy as jnp
from jax import lax
from jax.sharding import PartitionSpec as P

H = 128
TB = 512


def body(
    con_embed,
    var_embed,
    row_coef,
    col_coef,
    self_weight,
    msg_weight,
    timestep,
    tile_rows,
    tile_cols,
    pattern,
    cotangent,
):
    highest = lax.Precision.HIGHEST
    con_count = con_embed.shape[0]
    var_count = var_embed.shape[0]
    row_blocks = con_count * lax.axis_size("vg") // TB
    col_blocks = var_count * lax.axis_size("cg") // TB
    row_index = tile_rows.reshape(-1)
    col_index = tile_cols.reshape(-1)
    tile_count = row_index.shape[0]
    per_turn = math.gcd(tile_count, 8)
    turns = tile_count // per_turn
    patterns_here = pattern.reshape(turns, per_turn, TB, TB)
    row_turns = row_index.reshape(turns, per_turn)
    col_turns = col_index.reshape(turns, per_turn)
    local_proj = (
        jnp.dot(var_embed, msg_weight, precision=highest, preferred_element_type=jnp.float32)
        * col_coef[:, None]
    ).astype(jnp.bfloat16)
    projected = lax.all_gather(local_proj, "cg", axis=0, tiled=True)
    source_blocks = projected.reshape(col_blocks, TB, H)
    row_ids = jnp.arange(row_blocks, dtype=jnp.int32)
    col_ids = jnp.arange(col_blocks, dtype=jnp.int32)

    def forward_turn(running, inputs):
        rows_now, cols_now, tile_mask = inputs
        products = jnp.einsum(
            "grc,gch->grh", tile_mask, source_blocks[cols_now], preferred_element_type=jnp.float32
        )
        selector = (rows_now[None, :] == row_ids[:, None]).astype(jnp.float32)
        running = running + jnp.dot(
            selector,
            products.reshape(per_turn, TB * H),
            precision=highest,
            preferred_element_type=jnp.float32,
        )
        return (running, None)

    forward_sum, _ = lax.scan(
        forward_turn,
        jnp.zeros((row_blocks, TB * H), jnp.float32),
        (row_turns, col_turns, patterns_here),
    )
    messages = lax.psum_scatter(
        forward_sum.reshape(row_blocks * TB, H), "vg", scatter_dimension=0, tiled=True
    )
    frequency = jnp.exp(-math.log(10000.0) * jnp.arange(H // 2, dtype=jnp.float32) / (H // 2))
    phases = timestep[0].astype(jnp.float32) * frequency
    time_embed = jnp.concatenate([jnp.sin(phases), jnp.cos(phases)])
    preact = (
        jnp.dot(con_embed, self_weight, precision=highest, preferred_element_type=jnp.float32)
        + row_coef[:, None] * messages
        + time_embed[None, :]
    )
    sigmoid_z = jax.nn.sigmoid(preact)
    con_update = con_embed + preact * sigmoid_z
    grad_pre = cotangent * sigmoid_z * (1.0 + preact * (1.0 - sigmoid_z))
    grad_con = cotangent + jnp.dot(
        grad_pre, self_weight.T, precision=highest, preferred_element_type=jnp.float32
    )
    local_self = jnp.dot(
        con_embed.T, grad_pre, precision=highest, preferred_element_type=jnp.float32
    )
    grad_messages = (row_coef[:, None] * grad_pre).astype(jnp.bfloat16)
    whole_rows = lax.all_gather(grad_messages, "vg", axis=0, tiled=True).reshape(row_blocks, TB, H)

    def backward_turn(running, inputs):
        rows_now, cols_now, tile_mask = inputs
        products = jnp.einsum(
            "grc,grh->gch", tile_mask, whole_rows[rows_now], preferred_element_type=jnp.float32
        )
        selector = (cols_now[None, :] == col_ids[:, None]).astype(jnp.float32)
        running = running + jnp.dot(
            selector,
            products.reshape(per_turn, TB * H),
            precision=highest,
            preferred_element_type=jnp.float32,
        )
        return (running, None)

    backward_sum, _ = lax.scan(
        backward_turn,
        jnp.zeros((col_blocks, TB * H), jnp.float32),
        (row_turns, col_turns, patterns_here),
    )
    grad_projected = lax.psum_scatter(
        backward_sum.reshape(col_blocks * TB, H), "cg", scatter_dimension=0, tiled=True
    )
    grad_lin = col_coef[:, None] * grad_projected
    grad_var = jnp.dot(
        grad_lin, msg_weight.T, precision=highest, preferred_element_type=jnp.float32
    )
    local_msg = jnp.dot(
        var_embed.T, grad_lin, precision=highest, preferred_element_type=jnp.float32
    )
    grad_msg, grad_self = lax.psum((local_msg, local_self), ("cg", "vg"))
    return (con_update, grad_con, grad_var, grad_msg, grad_self)


def solution(mesh):
    in_specs = (
        P(("cg", "vg"), None),
        P(("vg", "cg"), None),
        P(("cg", "vg")),
        P(("vg", "cg")),
        P(),
        P(),
        P(),
        P("cg", "vg", None),
        P("cg", "vg", None),
        P("cg", "vg", None, None, None),
        P(("cg", "vg"), None),
    )
    out_specs = (P(("cg", "vg"), None), P(("cg", "vg"), None), P(("vg", "cg"), None), P(), P())
    return jax.shard_map(body, mesh=mesh, in_specs=in_specs, out_specs=out_specs, check_vma=False)
```

profile of v0, /device:TPU:0, one launch (start us, length us, event | category | flops | bytes accessed | tf_op | source)
XLA Modules:
  0.0 396.2 jit_solution(18261910513397852142)
XLA Ops:
  7.2 0.0 all-gather.3.cloned.1.call-start
  7.2 1.0 copy-done
  8.2 2.1 fusion.31
  10.3 0.0 all-gather.3.cloned.1.call-update
  10.3 0.0 reduce-scatter.3.cloned.1.call-start
  10.4 0.5 broadcast.91
  10.9 1.3 reduce.6
  12.2 0.1 reshape_reshape.6
  12.3 1.3 reduce.7
  13.6 0.1 reshape_reshape.7
  13.7 48.8 %all-gather.3.cloned.1.call-done = bf16[8192,128]{1,0:T(8,128)(2,1)} async-done(((bf16[1024,128]{1,0:T(8,128)(2,1)}), bf16[8192,128]{1,0:T(8,128)(2,1)}) %all-gather.3.cloned.1.call-update) | async-done | bytes 2097168 | tf_op jit(solution)/shard_map/all_gather | solution.py:41
  62.5 22.9 %while.22 = (s32[]{:T(128)}, f32[8,65536]{1,0:T(8,128)}, s32[2,8]{1,0:T(2,128)S(1)}, bf16[2,8,512,512]{3,2,1,0:T(8,128)(2,1)}, s32[2,8]{1,0:T(2,128)S(1)}, /*ind...) while((s32[]{:T(128)}, f32[8,65536]{1,0:T(8,128)}, s32[2,8]{1,0:T(2,128)S(1)}, ...), condition=%wide.region_1.2_spmd.clone, body=%wide.region_0.1_spmd.clone.sunk | while | flops 588252224 | bytes 15733575 | solution.py:60
  62.5 3.2 gather_fusion
  65.8 3.7 fusion.65
  69.5 3.6 convolution_add_fusion.6
  73.2 3.2 gather_fusion
  76.4 3.7 fusion.65
  80.2 5.2 %convolution_add_fusion.6 = f32[8,65536]{1,0:T(8,128)} fusion(f32[1,8,512,128]{3,2,1,0:T(8,128)S(1)} %fusion.65, f32[8,65536]{1,0:T(8,128)} %get-tuple-element.252, pred[]{:T(512)S(6)} %compare.6, s32[8]{0:T(128)S(1)} %fusion.66), kind=kOutput, calls=%fused_computation.4.clone.1 | convolution fusion | flops 51380288 | bytes 6291489 | tf_op jit(solution)/shard_map/while/body/eval_jaxpr/dot_general | solution.py:52
  85.4 3.2 reshape.95
  88.6 0.0 reduce-scatter.3.cloned.1.call-update
  88.7 0.0 all-gather.5.cloned.1.call-start
  89.5 0.1 pad_maximum_fusion
  89.6 28.9 %reduce-scatter.3.cloned.1.call-done = f32[1024,128]{1,0:T(8,128)} async-done(((f32[4096,128]{1,0:T(8,128)}), f32[1024,128]{1,0:T(8,128)}) %reduce-scatter.3.cloned.1.call-update) | async-done | bytes 524304 | tf_op jit(solution)/shard_map/reduce_scatter | solution.py:65
  118.5 2.9 multiply_convert_fusion
  121.4 0.0 all-gather.5.cloned.1.call-update
  121.4 0.0 reduce-scatter.5.cloned.1.call-start
  121.5 12.3 %copy.16 = bf16[1,1,16,512,512]{3,4,2,1,0:T(8,128)(2,1)} copy(bf16[1,1,16,512,512]{4,3,2,1,0:T(8,128)(2,1)} %bitcast.88) | data formatting | bytes 16777216 | tf_op args[9]
  133.8 4.5 %all-gather.5.cloned.1.call-done = bf16[4096,128]{1,0:T(8,128)(2,1)} async-done(((bf16[1024,128]{1,0:T(8,128)(2,1)}), bf16[4096,128]{1,0:T(8,128)(2,1)}) %all-gather.5.cloned.1.call-update) | async-done | bytes 1048592 | tf_op jit(solution)/shard_map/all_gather | solution.py:86
  138.3 25.2 %while.23 = (s32[]{:T(128)}, f32[16,65536]{1,0:T(8,128)}, s32[2,8]{1,0:T(2,128)S(1)}, bf16[2,8,512,512]{2,3,1,0:T(8,128)(2,1)}, s32[2,8]{1,0:T(2,128)S(1)}, /*in...) while((s32[]{:T(128)}, f32[16,65536]{1,0:T(8,128)}, s32[2,8]{1,0:T(2,128)S(1)}, ...), condition=%wide.region_4.5_spmd.clone, body=%wide.region_3.4_spmd.clone.sunk | while | flops 639632512 | bytes 19927880 | solution.py:102
  138.3 2.9 gather_fusion.1
  141.2 3.7 fusion.71
  144.9 4.9 %convolution_add_fusion.7 = f32[16,65536]{1,0:T(8,128)} fusion(f32[16,65536]{1,0:T(8,128)} %get-tuple-element.276, f32[1,8,512,128]{3,2,1,0:T(8,128)S(1)} %fusion.71, pred[]{:T(512)S(6)} %compare.7, s32[8]{0:T(128)S(1)} %fusion.72), kind=kOutput, calls=%fused_computation.21.clone.1 | convolution fusion | flops 102760576 | bytes 10485793 | tf_op jit(solution)/shard_map/while/body/eval_jaxpr/dot_general | solution.py:94
  149.8 2.9 gather_fusion.1
  152.7 3.7 fusion.71
  156.5 7.1 %convolution_add_fusion.7 = f32[16,65536]{1,0:T(8,128)} fusion(f32[16,65536]{1,0:T(8,128)} %get-tuple-element.276, f32[1,8,512,128]{3,2,1,0:T(8,128)S(1)} %fusion.71, pred[]{:T(512)S(6)} %compare.7, s32[8]{0:T(128)S(1)} %fusion.72), kind=kOutput, calls=%fused_computation.21.clone.1 | convolution fusion | flops 102760576 | bytes 10485793 | tf_op jit(solution)/shard_map/while/body/eval_jaxpr/dot_general | solution.py:94
  163.5 3.9 reshape.97
  167.4 0.0 reduce-scatter.5.cloned.1.call-update
  167.4 0.2 all-reduce.3.cloned.1.call-start
  167.7 0.8 copy-done.5
  168.4 0.2 copy-done.8
  168.6 1.7 convolution_bitcast_fusion
  170.3 1.5 convolution_add_fusion.2
  171.9 84.1 %reduce-scatter.5.cloned.1.call-done = f32[1024,128]{1,0:T(8,128)} async-done(((f32[8192,128]{1,0:T(8,128)}), f32[1024,128]{1,0:T(8,128)}) %reduce-scatter.5.cloned.1.call-update) | async-done | bytes 524304 | tf_op jit(solution)/shard_map/reduce_scatter | solution.py:107
  256.0 2.8 convolution_bitcast_fusion.1
  258.8 2.5 fusion.33
  261.3 125.3 %all-reduce.3.cloned.1.call-done = (f32[128,128]{0,1:T(8,128)}, f32[128,128]{0,1:T(8,128)}) async-done(((f32[128,128]{0,1:T(8,128)}, f32[128,128]{0,1:T(8,128)}), (f32[128,128]{0,1:T(8,128)}, f32[128,128]{0,1:T(8,128)})) %all-reduce.3.cloned.1.call-update) | async-done | bytes 131088 | tf_op jit(solution)/shard_map/psum | solution.py:117
  386.6 1.6 copy.18
  388.1 1.6 copy.19
  (31 shorter events, 0.2 us)
Async XLA Ops:
  7.2 1.0 copy-start
  7.2 55.3 %all-gather.3.cloned.1.call-start = ((), (), s32[]{:S(2)}) async-start(), calls=%async_computation.2 | async-start | bytes 2359296 | tf_op jit(solution)/shard_map/all_gather | solution.py:41
  10.3 108.2 %reduce-scatter.3.cloned.1.call-start = ((), (), s32[]{:S(2)}) async-start(), calls=%async_computation.3 | async-start | bytes 2621440 | tf_op jit(solution)/shard_map/reduce_scatter | solution.py:65
  88.6 29.9 %copy-start.3 = (f32[1024,128]{1,0:T(8,128)S(1)}, f32[1024,128]{1,0:T(8,128)}, u32[]{:S(2)}) copy-start(f32[1024,128]{1,0:T(8,128)} %param.15) | copy-start | bytes 1572868
  88.6 29.9 %copy-start.4 = (f32[1024,128]{1,0:T(8,128)S(1)}, f32[1024,128]{1,0:T(8,128)}, u32[]{:S(2)}) copy-start(f32[1024,128]{1,0:T(8,128)} %param.25) | copy-start | bytes 1572868
  88.6 29.9 %copy-start.6 = (f32[128,128]{1,0:T(8,128)S(1)}, f32[128,128]{1,0:T(8,128)}, u32[]{:S(2)}) copy-start(f32[128,128]{1,0:T(8,128)} %param.19) | copy-start | bytes 196612
  88.6 29.9 %copy-start.7 = (f32[1024]{0:T(1024)S(1)}, f32[1024]{0:T(1024)}, u32[]{:S(2)}) copy-start(f32[1024]{0:T(1024)} %param.17) | copy-start | bytes 12292
  88.7 49.6 %all-gather.5.cloned.1.call-start = ((), (), s32[]{:S(2)}) async-start(), calls=%async_computation.4 | async-start | bytes 1310720 | tf_op jit(solution)/shard_map/all_gather | solution.py:86
  121.4 134.5 %reduce-scatter.5.cloned.1.call-start = ((), (), s32[]{:S(2)}) async-start(), calls=%async_computation.5 | async-start | bytes 4718592 | tf_op jit(solution)/shard_map/reduce_scatter | solution.py:107
  167.4 1.0 copy-start.5
  167.4 1.2 copy-start.8
  167.4 219.2 %all-reduce.3.cloned.1.call-start = ((), (), s32[]{:S(2)}) async-start(), calls=%async_computation.6 | async-start | bytes 262144 | tf_op jit(solution)/shard_map/psum | solution.py:117
  170.3 85.6 %copy-start.2 = (f32[1024]{0:T(1024)S(1)}, f32[1024]{0:T(1024)}, u32[]{:S(2)}) copy-start(f32[1024]{0:T(1024)} %param.18) | copy-start | bytes 12292
  170.3 88.5 %copy-start.1 = (f32[128,128]{1,0:T(8,128)S(1)}, f32[128,128]{1,0:T(8,128)}, u32[]{:S(2)}) copy-start(f32[128,128]{1,0:T(8,128)} %param.20) | copy-start | bytes 196612
Sparse Core Ops, SparseCore 0:
  10.7 51.7 all-gather.2
  88.8 29.6 reduce-scatter.2
  121.5 16.7 all-gather.4
  167.5 88.3 reduce-scatter.4
  262.1 124.4 all-reduce.2
where the time goes:
time: 397 us; the launch traced here: 396 us
  waiting for transfers between devices  292 us (74%)
  matrix products  49.2 us (12%)
  local copies, waits for them, and re-layouts  37.4 us (9%)
  between operations  14.6 us (4%)
    psum x1, waiting for transfers between devices, body(): grad_msg, grad_self = lax.psum((local_msg, local_self), ('cg', 'vg'))  125 us
    reduce_scatter x1, waiting for transfers between devices, body(): lax.psum_scatter(backward_sum.reshape(col_blocks * TB, H), 'cg', scatter_...  84.1 us
    all_gather x1, waiting for transfers between devices, body(): projected = lax.all_gather(local_proj, 'cg', axis=0, tiled=True)  48.8 us
    reduce_scatter x1, waiting for transfers between devices, body(): lax.psum_scatter(forward_sum.reshape(row_blocks * TB, H), 'vg', scatter_d...  28.9 us
    unnamed x22, local copies, waits for them, and re-layouts  17.9 us
    dot_general x2, matrix products, backward_turn(): jnp.dot(selector, products.reshape(per_turn, TB * H), precision=highest,...  12 us
    dot_general x2, matrix products, forward_turn(): jnp.dot(selector, products.reshape(per_turn, TB * H), precision=highest,...  8.83 us
  transfers between devices with their start and end apart: 5, of which 5 were waited for; matrix products, arithmetic and copies ran while one was open for 5% of the time, Pallas kernels for 0%

commit v1 on v0

--- a/solution.py
+++ b/solution.py
@@ -114,7 +114,7 @@
     local_msg = jnp.dot(
         var_embed.T, grad_lin, precision=highest, preferred_element_type=jnp.float32
     )
-    grad_msg, grad_self = lax.psum((local_msg, local_self), ("cg", "vg"))
+    grad_msg, grad_self = lax.psum(lax.psum((local_msg, local_self), "cg"), "vg")
     return (con_update, grad_con, grad_var, grad_msg, grad_self)
 
 

time: 397 us -> 374 us (0.942)
  waiting for transfers between devices: 292 us -> 269 us
    psum x1 -> x2, waiting for transfers between devices: 125 us -> 101 us  [the longest x1 69.7 us: body(): lax.psum((local_msg, local_self), 'cg')]
    unnamed x22 -> x24, local copies, waits for them, and re-layouts: 17.9 us -> 18 us
  transfers between devices with their start and end apart: 5 -> 6, of which waited for: 5 -> 6; matrix products, arithmetic and copies ran while one was open for 5% -> 5% of each run, Pallas kernels for 0% -> 0%
where the time goes in v1:
time: 374 us; the launch traced here: 373 us
  waiting for transfers between devices  269 us (72%)
  matrix products  48.3 us (13%)
  local copies, waits for them, and re-layouts  37.5 us (10%)
  between operations  14.9 us (4%)
    reduce_scatter x1, waiting for transfers between devices, body(): lax.psum_scatter(backward_sum.reshape(col_blocks * TB, H), 'cg', scatter_...  85.6 us
    psum x1, waiting for transfers between devices, body(): lax.psum((local_msg, local_self), 'cg')  69.7 us
    all_gather x1, waiting for transfers between devices, body(): projected = lax.all_gather(local_proj, 'cg', axis=0, tiled=True)  48.8 us
    psum x1, waiting for transfers between devices, body(): lax.psum(lax.psum((local_msg, local_self), 'cg'), 'vg')  31.7 us
    reduce_scatter x1, waiting for transfers between devices, body(): lax.psum_scatter(forward_sum.reshape(row_blocks * TB, H), 'vg', scatter_d...  28.9 us
    unnamed x24, local copies, waits for them, and re-layouts  18 us
    dot_general x2, matrix products, backward_turn(): jnp.dot(selector, products.reshape(per_turn, TB * H), precision=highest,...  12 us
    dot_general x2, matrix products, forward_turn(): jnp.dot(selector, products.reshape(per_turn, TB * H), precision=highest,...  8.83 us
  transfers between devices with their start and end apart: 6, of which 6 were waited for; matrix products, arithmetic and copies ran while one was open for 5% of the time, Pallas kernels for 0%

profile of v1, /device:TPU:0, one launch (start us, length us, event | category | flops | bytes accessed | tf_op | source)
XLA Modules:
  0.0 373.4 jit_solution(15085152680779271917)
XLA Ops:
  7.2 0.0 all-gather.3.cloned.1.call-start
  7.2 1.0 copy-done
  8.2 2.1 fusion.31
  10.3 0.0 all-gather.3.cloned.1.call-update
  10.3 0.0 reduce-scatter.3.cloned.1.call-start
  10.4 0.5 broadcast.91
  10.9 1.3 reduce.6
  12.2 0.1 reshape_reshape.6
  12.3 1.3 reduce.7
  13.6 0.1 reshape_reshape.7
  13.7 48.8 %all-gather.3.cloned.1.call-done = bf16[8192,128]{1,0:T(8,128)(2,1)} async-done(((bf16[1024,128]{1,0:T(8,128)(2,1)}), bf16[8192,128]{1,0:T(8,128)(2,1)}) %all-gather.3.cloned.1.call-update) | async-done | bytes 2097168 | tf_op jit(solution)/shard_map/all_gather | solution.py:41
  62.5 22.9 %while.22 = (s32[]{:T(128)}, f32[8,65536]{1,0:T(8,128)}, s32[2,8]{1,0:T(2,128)S(1)}, bf16[2,8,512,512]{3,2,1,0:T(8,128)(2,1)}, s32[2,8]{1,0:T(2,128)S(1)}, /*ind...) while((s32[]{:T(128)}, f32[8,65536]{1,0:T(8,128)}, s32[2,8]{1,0:T(2,128)S(1)}, ...), condition=%wide.region_1.2_spmd.clone, body=%wide.region_0.1_spmd.clone.sunk | while | flops 588252224 | bytes 15733575 | solution.py:60
  62.5 3.2 gather_fusion
  65.8 3.7 fusion.65
  69.5 3.6 convolution_add_fusion.6
  73.2 3.2 gather_fusion
  76.4 3.7 fusion.65
  80.2 5.2 %convolution_add_fusion.6 = f32[8,65536]{1,0:T(8,128)} fusion(f32[1,8,512,128]{3,2,1,0:T(8,128)S(1)} %fusion.65, f32[8,65536]{1,0:T(8,128)} %get-tuple-element.254, pred[]{:T(512)S(6)} %compare.6, s32[8]{0:T(128)S(1)} %fusion.66), kind=kOutput, calls=%fused_computation.4.clone.1 | convolution fusion | flops 51380288 | bytes 6291489 | tf_op jit(solution)/shard_map/while/body/eval_jaxpr/dot_general | solution.py:52
  85.4 3.2 reshape.95
  88.7 0.0 reduce-scatter.3.cloned.1.call-update
  88.7 0.0 all-gather.5.cloned.1.call-start
  89.5 0.1 pad_maximum_fusion
  89.6 28.9 %reduce-scatter.3.cloned.1.call-done = f32[1024,128]{1,0:T(8,128)} async-done(((f32[4096,128]{1,0:T(8,128)}), f32[1024,128]{1,0:T(8,128)}) %reduce-scatter.3.cloned.1.call-update) | async-done | bytes 524304 | tf_op jit(solution)/shard_map/reduce_scatter | solution.py:65
  118.5 2.9 multiply_convert_fusion
  121.4 0.0 reduce-scatter.5.cloned.1.call-start
  121.5 12.3 %copy.16 = bf16[1,1,16,512,512]{3,4,2,1,0:T(8,128)(2,1)} copy(bf16[1,1,16,512,512]{4,3,2,1,0:T(8,128)(2,1)} %bitcast.88) | data formatting | bytes 16777216 | tf_op args[9]
  133.8 4.4 %all-gather.5.cloned.1.call-done = bf16[4096,128]{1,0:T(8,128)(2,1)} async-done(((bf16[1024,128]{1,0:T(8,128)(2,1)}), bf16[4096,128]{1,0:T(8,128)(2,1)}) %all-gather.5.cloned.1.call-update) | async-done | bytes 1048592 | tf_op jit(solution)/shard_map/all_gather | solution.py:86
  138.3 25.3 %while.23 = (s32[]{:T(128)}, f32[16,65536]{1,0:T(8,128)}, s32[2,8]{1,0:T(2,128)S(1)}, bf16[2,8,512,512]{2,3,1,0:T(8,128)(2,1)}, s32[2,8]{1,0:T(2,128)S(1)}, /*in...) while((s32[]{:T(128)}, f32[16,65536]{1,0:T(8,128)}, s32[2,8]{1,0:T(2,128)S(1)}, ...), condition=%wide.region_4.5_spmd.clone, body=%wide.region_3.4_spmd.clone.sunk | while | flops 639632512 | bytes 19927880 | solution.py:102
  138.3 2.9 gather_fusion.1
  141.2 3.7 fusion.71
  144.9 4.9 %convolution_add_fusion.7 = f32[16,65536]{1,0:T(8,128)} fusion(f32[16,65536]{1,0:T(8,128)} %get-tuple-element.278, f32[1,8,512,128]{3,2,1,0:T(8,128)S(1)} %fusion.71, pred[]{:T(512)S(6)} %compare.7, s32[8]{0:T(128)S(1)} %fusion.72), kind=kOutput, calls=%fused_computation.21.clone.1 | convolution fusion | flops 102760576 | bytes 10485793 | tf_op jit(solution)/shard_map/while/body/eval_jaxpr/dot_general | solution.py:94
  149.8 2.9 gather_fusion.1
  152.7 3.7 fusion.71
  156.5 7.1 %convolution_add_fusion.7 = f32[16,65536]{1,0:T(8,128)} fusion(f32[16,65536]{1,0:T(8,128)} %get-tuple-element.278, f32[1,8,512,128]{3,2,1,0:T(8,128)S(1)} %fusion.71, pred[]{:T(512)S(6)} %compare.7, s32[8]{0:T(128)S(1)} %fusion.72), kind=kOutput, calls=%fused_computation.21.clone.1 | convolution fusion | flops 102760576 | bytes 10485793 | tf_op jit(solution)/shard_map/while/body/eval_jaxpr/dot_general | solution.py:94
  163.5 3.9 %reshape.97 = f32[8192,128]{1,0:T(8,128)} reshape(f32[16,65536]{1,0:T(8,128)} %get-tuple-element.80) | data formatting | bytes 8388608 | tf_op jit(solution)/shard_map/reshape | solution.py:108
  167.4 0.2 all-reduce.5.cloned.1.call-start
  167.7 0.8 copy-done.6
  168.4 0.2 copy-done.9
  168.6 1.7 convolution_bitcast_fusion
  170.4 85.6 %reduce-scatter.5.cloned.1.call-done = f32[1024,128]{1,0:T(8,128)} async-done(((f32[8192,128]{1,0:T(8,128)}), f32[1024,128]{1,0:T(8,128)}) %reduce-scatter.5.cloned.1.call-update) | async-done | bytes 524304 | tf_op jit(solution)/shard_map/reduce_scatter | solution.py:107
  256.0 2.9 convolution_bitcast_fusion.1
  258.9 0.0 all-reduce.7.cloned.1.call-start
  259.0 1.5 convolution_add_fusion.2
  260.5 69.7 %all-reduce.5.cloned.1.call-done = (f32[128,128]{0,1:T(8,128)}, f32[128,128]{0,1:T(8,128)}) async-done(((f32[128,128]{0,1:T(8,128)}, f32[128,128]{0,1:T(8,128)}), (f32[128,128]{0,1:T(8,128)}, f32[128,128]{0,1:T(8,128)})) %all-reduce.5.cloned.1.call-update) | async-done | bytes 131088 | tf_op jit(solution)/shard_map/psum | solution.py:117
  330.3 1.4 fusion.33
  331.7 31.7 %all-reduce.7.cloned.1.call-done = (f32[128,128]{0,1:T(8,128)}, f32[128,128]{0,1:T(8,128)}) async-done(((f32[128,128]{0,1:T(8,128)}, f32[128,128]{0,1:T(8,128)}), (f32[128,128]{0,1:T(8,128)}, f32[128,128]{0,1:T(8,128)})) %all-reduce.7.cloned.1.call-update) | async-done | bytes 131088 | tf_op jit(solution)/shard_map/psum | solution.py:117
  363.4 1.6 copy.18
  365.0 1.6 copy.19
  (36 shorter events, 0.3 us)
Async XLA Ops:
  7.2 1.0 copy-start
  7.2 55.3 %all-gather.3.cloned.1.call-start = ((), (), s32[]{:S(2)}) async-start(), calls=%async_computation.2 | async-start | bytes 2359296 | tf_op jit(solution)/shard_map/all_gather | solution.py:41
  10.3 108.2 %reduce-scatter.3.cloned.1.call-start = ((), (), s32[]{:S(2)}) async-start(), calls=%async_computation.3 | async-start | bytes 2621440 | tf_op jit(solution)/shard_map/reduce_scatter | solution.py:65
  88.6 29.9 %copy-start.4 = (f32[1024,128]{1,0:T(8,128)S(1)}, f32[1024,128]{1,0:T(8,128)}, u32[]{:S(2)}) copy-start(f32[1024,128]{1,0:T(8,128)} %param.15) | copy-start | bytes 1572868
  88.6 29.9 %copy-start.5 = (f32[1024,128]{1,0:T(8,128)S(1)}, f32[1024,128]{1,0:T(8,128)}, u32[]{:S(2)}) copy-start(f32[1024,128]{1,0:T(8,128)} %param.25) | copy-start | bytes 1572868
  88.6 29.9 %copy-start.7 = (f32[128,128]{1,0:T(8,128)S(1)}, f32[128,128]{1,0:T(8,128)}, u32[]{:S(2)}) copy-start(f32[128,128]{1,0:T(8,128)} %param.19) | copy-start | bytes 196612
  88.6 29.9 %copy-start.8 = (f32[1024]{0:T(1024)S(1)}, f32[1024]{0:T(1024)}, u32[]{:S(2)}) copy-start(f32[1024]{0:T(1024)} %param.17) | copy-start | bytes 12292
  88.7 49.6 %all-gather.5.cloned.1.call-start = ((), (), s32[]{:S(2)}) async-start(), calls=%async_computation.4 | async-start | bytes 1310720 | tf_op jit(solution)/shard_map/all_gather | solution.py:86
  121.4 134.5 %reduce-scatter.5.cloned.1.call-start = ((), (), s32[]{:S(2)}) async-start(), calls=%async_computation.5 | async-start | bytes 4718592 | tf_op jit(solution)/shard_map/reduce_scatter | solution.py:107
  167.4 1.0 copy-start.6
  167.4 1.2 copy-start.9
  167.4 88.5 %copy-start.3 = (f32[1024]{0:T(1024)S(1)}, f32[1024]{0:T(1024)}, u32[]{:S(2)}) copy-start(f32[1024]{0:T(1024)} %param.18) | copy-start | bytes 12292
  167.4 162.8 %all-reduce.5.cloned.1.call-start = ((), (), s32[]{:S(2)}) async-start(), calls=%async_computation.6 | async-start | bytes 262144 | tf_op jit(solution)/shard_map/psum | solution.py:117
  170.3 159.9 %copy-start.2 = (f32[128,128]{1,0:T(8,128)S(1)}, f32[128,128]{1,0:T(8,128)}, u32[]{:S(2)}) copy-start(f32[128,128]{1,0:T(8,128)} %param.20) | copy-start | bytes 196612
  256.0 74.3 %copy-start.1 = (f32[1024,128]{1,0:T(8,128)S(1)}, f32[1024,128]{1,0:T(8,128)}, u32[]{:S(2)}) copy-start(f32[1024,128]{1,0:T(8,128)} %reduce-scatter.5.cloned.1.call-done) | copy-start | bytes 1572868
  258.9 104.5 %all-reduce.7.cloned.1.call-start = ((), (), s32[]{:S(2)}) async-start(), calls=%async_computation.7 | async-start | bytes 262144 | tf_op jit(solution)/shard_map/psum | solution.py:117
Sparse Core Ops, SparseCore 0:
  10.7 51.7 all-gather.2
  88.8 29.6 reduce-scatter.2
  121.5 16.6 all-gather.4
  167.6 88.3 reduce-scatter.4
  259.9 70.3 all-reduce.4
  332.5 30.9 all-reduce.6
